TPU v7x, 256 devices: a whole 4x4x8 slice. The times are simulated.
256 devices in a mesh: wide: 32 (over z, x), narrow: 8 (over y, core).
Axes of the slice: x: 4, y: 4, z: 8, core: 2. Of those that a mesh axis runs over, the one named last changes fastest.
Arguments:
- hidden_in: bfloat16 [4096, 2048], P(('wide', 'narrow')), may hold values from -6 to 6
- queries: bfloat16 [4096, 2048], P(('wide', 'narrow')), may hold values from -6 to 6
- cache_key: bfloat16 [4096, 128, 256], P(('wide', 'narrow')), may hold values from -6 to 6
- cache_value: bfloat16 [4096, 128, 256], P(('wide', 'narrow')), may hold values from -6 to 6
- new_key: bfloat16 [4096, 256], P(('wide', 'narrow')), may hold values from -6 to 6
- new_value: bfloat16 [4096, 256], P(('wide', 'narrow')), may hold values from -6 to 6
- lengths: int32 [4096], P(('wide', 'narrow')), may hold values from 2 to 128, as said below
- norm_gain: bfloat16 [2048], replicated, may hold values from 0.5 to 1.5
- gate_codes: bfloat16 [256, 2048, 384], P(('wide', 'narrow')), may hold values from -4 to 4
- gate_scale: float32 [256, 16, 3], P(('wide', 'narrow')), may hold values from 0.011048543 to 0.044194173
- up_codes: bfloat16 [256, 2048, 384], P(('wide', 'narrow')), may hold values from -4 to 4
- up_scale: float32 [256, 16, 3], P(('wide', 'narrow')), may hold values from 0.011048543 to 0.044194173
- down_codes: bfloat16 [256, 384, 2048], P(('wide', 'narrow')), may hold values from -4 to 4
- down_scale: float32 [256, 3, 16], P(('wide', 'narrow')), may hold values from 0.018042196 to 0.07216878
- think_ids: int32 [4096, 8], P(('wide', 'narrow')), may hold values from 0 to 127, all different within a row; in each aligned block of 16 rows (0 to 15, 16 to 31, ...) at most 2 rows name the same one
- think_gates: float32 [4096, 8], P(('wide', 'narrow')), may hold values from 0.05 to 0.3
- talker_source: int32 [4096], P(('wide', 'narrow')), may hold values from 0 to 4095, as said below
- talker_gain: bfloat16 [2048], replicated, may hold values from 0.5 to 1.5
- talk_gate_w: bfloat16 [8, 2048, 384], P('narrow'), may hold values from -0.125 to 0.125
- talk_up_w: bfloat16 [8, 2048, 384], P('narrow'), may hold values from -0.125 to 0.125
- talk_down_w: bfloat16 [8, 384, 1024], P('narrow'), may hold values from -0.3125 to 0.3125
- talk_ids: int32 [4096, 2], P(('wide', 'narrow')), may hold values from 0 to 7, all different within a row; in each aligned block of 16 rows (0 to 15, 16 to 31, ...) at most 8 rows name the same one
- talk_gates: float32 [4096, 2], P(('wide', 'narrow')), may hold values from 0.3 to 0.7
Outputs:
- thinker_out: bfloat16 [4096, 2048], P(('wide', 'narrow'))
- talker_out: bfloat16 [4096, 1024], P(('wide', 'narrow'))
Inputs may be any that keep to these rules, and one draw needn't show every extreme that they name: `think_ids`: each row names 8 different thinker experts; among the rows of one device no expert is named by more than 2 rows. `talk_ids`: each position names 2 different talker experts; among the positions of one device no expert is named by more than 8. `lengths`: some row uses all 128 cached positions. `talker_source`: A permutation of the rows. The row feeding a talker position lies on the same narrow index as the position. The rows of one device feed positions on exactly 16 devices, 1 positions on each.
All inputs are finite; a program needn't handle non-finite values.
Results may differ from a plain program's by a relative error of at most 0.018.
Values may be sent and summed in bfloat16 or wider, within the bound.
No kernel may reach another device: no remote copies, remote signals or barrier semaphores. Data moves between devices by JAX's collectives and lax.ppermute only.
A program may use at most 64 MiB of HBM per device.

v0:
```python
import jax
import jax.numpy as jnp
from jax import lax
from jax.sharding import PartitionSpec as P

HEADS = 16
KV_HEADS = 2
HEAD_DIM = 128
BLK = 128
TOP = 8
TTOP = 2
EPSILON = 1e-06


def dequantize(code_block, scale_block):
    height, breadth = code_block.shape
    tiles = code_block.astype(jnp.float32).reshape(height // BLK, BLK, breadth // BLK, BLK)
    tiles = tiles * scale_block[:, None, :, None]
    return tiles.reshape(height, breadth).astype(jnp.bfloat16)


def rms_norm(values, gain):
    values = values.astype(jnp.float32)
    spread = jnp.mean(values * values, axis=-1, keepdims=True)
    return (values * lax.rsqrt(spread + EPSILON) * gain.astype(jnp.float32)).astype(jnp.bfloat16)


def swiglu(inputs, gate_dense, up_dense, down_dense):
    gated = jnp.dot(inputs, gate_dense, preferred_element_type=jnp.float32)
    lifted = jnp.dot(inputs, up_dense, preferred_element_type=jnp.float32)
    middle = (jax.nn.silu(gated) * lifted).astype(jnp.bfloat16)
    return jnp.dot(middle, down_dense, preferred_element_type=jnp.float32).astype(jnp.bfloat16)


def attend(queries, cache_key, cache_value, new_key, new_value, lengths):
    row_count = queries.shape[0]
    positions = cache_key.shape[1]
    groups = HEADS // KV_HEADS
    scaling = HEAD_DIM ** (-0.5)
    asked = queries.reshape(row_count, KV_HEADS, groups, HEAD_DIM)
    cached_keys = cache_key.reshape(row_count, positions, KV_HEADS, HEAD_DIM)
    cached_values = cache_value.reshape(row_count, positions, KV_HEADS, HEAD_DIM)
    scores = (
        jnp.einsum("rkgd,rtkd->rkgt", asked, cached_keys, preferred_element_type=jnp.float32)
        * scaling
    )
    newest_key = new_key.reshape(row_count, KV_HEADS, HEAD_DIM)
    fresh_score = (
        jnp.einsum("rkgd,rkd->rkg", asked, newest_key, preferred_element_type=jnp.float32) * scaling
    )
    places = jnp.arange(positions, dtype=jnp.int32)
    live_mask = places[None, :] < lengths[:, None]
    scores = jnp.where(live_mask[:, None, None, :], scores, -jnp.inf)
    highest = jnp.maximum(jnp.max(scores, axis=-1), fresh_score)
    weights = jnp.exp(scores - highest[..., None])
    own_weight = jnp.exp(fresh_score - highest)
    totals = jnp.sum(weights, axis=-1) + own_weight
    probabilities = (weights / totals[..., None]).astype(jnp.bfloat16)
    own_prob = (own_weight / totals).astype(jnp.bfloat16)
    mixture = jnp.einsum(
        "rkgt,rtkd->rkgd", probabilities, cached_values, preferred_element_type=jnp.float32
    )
    newest = new_value.reshape(row_count, KV_HEADS, 1, HEAD_DIM).astype(jnp.float32)
    mixture = mixture + own_prob.astype(jnp.float32)[..., None] * newest
    return mixture.reshape(row_count, HEADS * HEAD_DIM)


def slot_tables(expert_ids, gate_weights, expert_count, capacity):
    chosen = expert_ids[:, :, None] == jnp.arange(expert_count, dtype=jnp.int32)[None, None, :]
    picked = jnp.any(chosen, axis=1).astype(jnp.int32)
    weight_of = jnp.sum(jnp.where(chosen, gate_weights[:, :, None], jnp.float32(0.0)), axis=1)
    ranks = jnp.cumsum(picked, axis=0) - picked
    onehot = (picked[:, :, None] == 1) & (
        ranks[:, :, None] == jnp.arange(capacity, dtype=jnp.int32)[None, None, :]
    )
    placing = jnp.transpose(onehot, (1, 2, 0))
    return (placing, weight_of)


def local(
    hidden_in,
    queries,
    cache_key,
    cache_value,
    new_key,
    new_value,
    lengths,
    norm_gain,
    gate_codes,
    gate_scale,
    up_codes,
    up_scale,
    down_codes,
    down_scale,
    think_ids,
    think_gates,
    talker_source,
    talker_gain,
    talk_gate_w,
    talk_up_w,
    talk_down_w,
    talk_ids,
    talk_gates,
):
    wide_count = lax.axis_size("wide")
    narrow_count = lax.axis_size("narrow")
    row_count = hidden_in.shape[0]
    breadth = hidden_in.shape[1]
    attended = attend(queries, cache_key, cache_value, new_key, new_value, lengths)
    residual = hidden_in.astype(jnp.float32) + attended
    normed = rms_norm(residual, norm_gain)
    experts = wide_count * narrow_count // 2
    capacity = min(row_count, max(2, 2 * row_count * TOP // experts))
    placing, weight_of = slot_tables(think_ids, think_gates, experts, capacity)
    outgoing = jnp.einsum(
        "ecr,rd->ecd", placing.astype(jnp.bfloat16), normed, preferred_element_type=jnp.float32
    ).astype(jnp.bfloat16)
    doubled = jnp.broadcast_to(outgoing[:, None], (experts, 2, capacity, breadth)).reshape(
        wide_count, narrow_count, capacity, breadth
    )
    arrived = lax.all_to_all(
        lax.all_to_all(doubled, "wide", split_axis=0, concat_axis=0, tiled=True),
        "narrow",
        split_axis=1,
        concat_axis=1,
        tiled=True,
    )
    gate_dense = dequantize(gate_codes[0], gate_scale[0])
    up_dense = dequantize(up_codes[0], up_scale[0])
    down_dense = dequantize(down_codes[0], down_scale[0])
    produced = swiglu(arrived.reshape(-1, breadth), gate_dense, up_dense, down_dense)
    produced = produced.reshape(wide_count, narrow_count, capacity, breadth)
    returned = lax.all_to_all(
        lax.all_to_all(produced, "wide", split_axis=0, concat_axis=0, tiled=True),
        "narrow",
        split_axis=1,
        concat_axis=1,
        tiled=True,
    )
    paired = returned.reshape(experts, 2, capacity, breadth)
    summed = paired[:, 0].astype(jnp.float32) + paired[:, 1].astype(jnp.float32)
    combine = placing.astype(jnp.float32) * jnp.transpose(weight_of)[:, None, :]
    routed = jnp.einsum("ecr,ecd->rd", combine, summed, precision=lax.Precision.HIGHEST)
    thinker_out = (residual + routed).astype(jnp.bfloat16)
    own_wide = talker_source // row_count // narrow_count
    own_local = talker_source % row_count
    gathered = lax.all_gather(thinker_out, "wide", axis=0, tiled=True)
    talker_in = jnp.take(gathered, own_wide * row_count + own_local, axis=0)
    talker_normed = rms_norm(talker_in, talker_gain)
    talk_capacity = min(row_count, max(2, 2 * row_count * TTOP // narrow_count))
    talk_placing, talk_weight = slot_tables(talk_ids, talk_gates, narrow_count, talk_capacity)
    talk_outgoing = jnp.einsum(
        "ecr,rd->ecd",
        talk_placing.astype(jnp.bfloat16),
        talker_normed,
        preferred_element_type=jnp.float32,
    ).astype(jnp.bfloat16)
    incoming = lax.all_to_all(talk_outgoing, "narrow", split_axis=0, concat_axis=0, tiled=True)
    sources = incoming.shape[0]
    items = incoming.shape[1]
    result = swiglu(incoming.reshape(-1, breadth), talk_gate_w[0], talk_up_w[0], talk_down_w[0])
    talk_done = result.reshape(sources, items, -1)
    talk_back = lax.all_to_all(talk_done, "narrow", split_axis=0, concat_axis=0, tiled=True)
    talk_combine = talk_placing.astype(jnp.float32) * jnp.transpose(talk_weight)[:, None, :]
    talked = jnp.einsum(
        "ecr,ecd->rd", talk_combine, talk_back.astype(jnp.float32), precision=lax.Precision.HIGHEST
    )
    return (thinker_out, talked.astype(jnp.bfloat16))


def solution(mesh):
    return jax.shard_map(
        local,
        mesh=mesh,
        in_specs=(
            P(("wide", "narrow"), None),
            P(("wide", "narrow"), None),
            P(("wide", "narrow"), None, None),
            P(("wide", "narrow"), None, None),
            P(("wide", "narrow"), None),
            P(("wide", "narrow"), None),
            P(("wide", "narrow")),
            P(),
            P(("wide", "narrow"), None, None),
            P(("wide", "narrow"), None, None),
            P(("wide", "narrow"), None, None),
            P(("wide", "narrow"), None, None),
            P(("wide", "narrow"), None, None),
            P(("wide", "narrow"), None, None),
            P(("wide", "narrow"), None),
            P(("wide", "narrow"), None),
            P(("wide", "narrow")),
            P(),
            P("narrow", None, None),
            P("narrow", None, None),
            P("narrow", None, None),
            P(("wide", "narrow"), None),
            P(("wide", "narrow"), None),
        ),
        out_specs=(P(("wide", "narrow"), None), P(("wide", "narrow"), None)),
        check_vma=False,
    )
```

profile of v0, /device:TPU:1, one launch (start us, length us, event | category | flops | bytes accessed | tf_op | source)
XLA Modules:
  0.0 348.2 jit_solution(10771011624162334648)
XLA Ops:
  17.8 60.3 %all_to_all.30 = bf16[32,8,2,2048]{3,2,1,0:T(2,128)(2,1)S(1)} all-to-all(bf16[32,8,2,2048]{3,2,1,0:T(2,128)(2,1)S(1)} %bitcast.148), channel_id=1, replica_groups=mesh['wide'=32,'narrow'=8] {'wide'}, dimensions={0} | all-to-all | bytes 4194304 | tf_op jit(solution)/shard_map/all_to_all | solution.py:122
  78.1 3.1 copy.109
  81.2 7.4 %all-to-all-start.1 = ((bf16[32,8,2,2048]{3,2,0,1:T(2,128)(2,1)}), bf16[32,8,2,2048]{3,2,0,1:T(2,128)(2,1)}, u32[]{:S(2)}, u32[]{:S(2)}) async-start(bf16[32,8,2,2048]{3,2,0,1:T(2,128)(2,1)} %copy.109), calls=%async_computation.1 | async-start | bytes 4194304 | tf_op jit(solution)/shard_map/all_to_all | solution.py:121
  90.7 4.3 %copy.130 = f32[48,8,16,128]{3,2,1,0:T(8,128)} copy(f32[48,8,16,128]{3,1,2,0:T(8,128)} %bitcast.146) | data formatting | bytes 6291456
  95.1 2.1 copy.112
  97.2 2.7 copy.132
  101.9 13.0 %all-to-all-done.1 = bf16[32,8,2,2048]{3,2,0,1:T(2,128)(2,1)} async-done(((bf16[32,8,2,2048]{3,2,0,1:T(2,128)(2,1)}), bf16[32,8,2,2048]{3,2,0,1:T(2,128)(2,1)}, u32[]{:S(2)}, u32[]{:S(2)}) %all-to-all-start.1) | async-done | bytes 2097184 | tf_op jit(solution)/shard_map/all_to_all | solution.py:121
  114.9 5.2 %copy.110 = bf16[32,8,2,2048]{3,2,1,0:T(2,128)(2,1)} copy(bf16[32,8,2,2048]{3,2,0,1:T(2,128)(2,1)} %all-to-all-done.1) | data formatting | bytes 4194304 | tf_op jit(solution)/shard_map/all_to_all | solution.py:121
  120.1 4.1 %reshape.190 = bf16[512,2048]{1,0:T(8,128)(2,1)} reshape(bf16[32,8,2,2048]{3,2,1,0:T(2,128)(2,1)} %copy.110) | data formatting | bytes 4194304 | tf_op jit(solution)/shard_map/reshape | solution.py:131
  124.1 4.2 %fusion.8 = f32[512,384]{1,0:T(8,128)} fusion(bf16[512,2048]{1,0:T(8,128)(2,1)} %reshape.190, bf16[48,8,16,128]{3,2,1,0:T(8,128)(2,1)} %bitcast.152), kind=kOutput, calls=%fused_computation.16 | convolution fusion | flops 805306368 | bytes 4456448 | tf_op jit(solution)/shard_map/dot_general | solution.py:29
  130.3 7.1 %convolution_convert_fusion = bf16[512,2048]{1,0:T(8,128)(2,1)} fusion(f32[48,8,16,128]{3,2,1,0:T(8,128)} %bitcast.150, bf16[1,384,2048]{2,1,0:T(8,128)(2,1)} %param.35, bf16[512,2048]{1,0:T(8,128)(2,1)} %reshape.190, bf16[48,8,16,128]{3,2,1,0:T(8,128)(2,1)S(1)} %bitcast.151, f32[512,384]{1,0:T(8,128)} %fusion.8), kind=kOutput, calls=%fused_computation.5 | convolution fusion | flops 1615200256 | bytes 11272192 | tf_op jit(solution)/shard_map/dot_general | solution.py:32
  137.4 4.4 %reshape.191 = bf16[32,8,2,2048]{3,2,1,0:T(2,128)(2,1)} reshape(bf16[512,2048]{1,0:T(8,128)(2,1)} %convolution_convert_fusion) | data formatting | bytes 4194304 | tf_op jit(solution)/shard_map/reshape | solution.py:132
  141.8 53.8 %all_to_all.31 = bf16[32,8,2,2048]{3,2,1,0:T(2,128)(2,1)S(1)} all-to-all(bf16[32,8,2,2048]{3,2,1,0:T(2,128)(2,1)} %reshape.191), channel_id=1, replica_groups=mesh['wide'=32,'narrow'=8] {'wide'}, dimensions={0} | all-to-all | bytes 4194304 | tf_op jit(solution)/shard_map/all_to_all | solution.py:134
  195.6 3.1 copy.113
  198.7 7.3 %all-to-all-start.3 = ((bf16[32,8,2,2048]{3,2,0,1:T(2,128)(2,1)}), bf16[32,8,2,2048]{3,2,0,1:T(2,128)(2,1)}, u32[]{:S(2)}, u32[]{:S(2)}) async-start(bf16[32,8,2,2048]{3,2,0,1:T(2,128)(2,1)} %copy.113), calls=%async_computation.3 | async-start | bytes 4194304 | tf_op jit(solution)/shard_map/all_to_all | solution.py:133
  206.2 26.1 %all-to-all-done.3 = bf16[32,8,2,2048]{3,2,0,1:T(2,128)(2,1)} async-done(((bf16[32,8,2,2048]{3,2,0,1:T(2,128)(2,1)}), bf16[32,8,2,2048]{3,2,0,1:T(2,128)(2,1)}, u32[]{:S(2)}, u32[]{:S(2)}) %all-to-all-start.3) | async-done | bytes 2097184 | tf_op jit(solution)/shard_map/all_to_all | solution.py:133
  232.4 3.8 %copy.114 = bf16[32,8,2,2048]{3,2,1,0:T(2,128)(2,1)S(1)} copy(bf16[32,8,2,2048]{3,2,0,1:T(2,128)(2,1)} %all-to-all-done.3) | data formatting | bytes 4194304 | tf_op jit(solution)/shard_map/all_to_all | solution.py:133
  237.4 2.9 fusion.2
  240.7 68.5 %all-gather.2.cloned.1.call-done = bf16[512,2048]{1,0:T(8,128)(2,1)} async-done(((bf16[16,2048]{1,0:T(8,128)(2,1)}), bf16[512,2048]{1,0:T(8,128)(2,1)}) %all-gather.2.cloned.1.call-update) | async-done | bytes 2097168 | tf_op jit(solution)/shard_map/all_gather | solution.py:147
  309.2 2.5 gather_fusion
  312.2 15.9 %all_to_all.32 = bf16[8,8,2048]{2,1,0:T(8,128)(2,1)S(1)} all-to-all(bf16[8,8,2048]{2,1,0:T(8,128)(2,1)S(1)} %convolution_convert_fusion.2), channel_id=1, replica_groups=mesh['wide'=32,'narrow'=8] {'narrow'}, dimensions={0} | all-to-all | bytes 524288 | tf_op jit(solution)/shard_map/all_to_all | solution.py:158
  328.4 2.5 fusion.22
  330.9 4.3 %all-to-all-start.5 = ((bf16[8,8,1024]{2,1,0:T(8,128)(2,1)}), bf16[8,8,1024]{2,1,0:T(8,128)(2,1)S(1)}, u32[]{:S(2)}, u32[]{:S(2)}) async-start(bf16[8,8,1024]{2,1,0:T(8,128)(2,1)} %fusion.22), calls=%async_computation.5 | async-start | bytes 262144 | tf_op jit(solution)/shard_map/all_to_all | solution.py:163
  335.2 5.3 %all-to-all-done.5 = bf16[8,8,1024]{2,1,0:T(8,128)(2,1)S(1)} async-done(((bf16[8,8,1024]{2,1,0:T(8,128)(2,1)}), bf16[8,8,1024]{2,1,0:T(8,128)(2,1)S(1)}, u32[]{:S(2)}, u32[]{:S(2)}) %all-to-all-start.5) | async-done | bytes 131104 | tf_op jit(solution)/shard_map/all_to_all | solution.py:163
  (84 shorter events, 19.9 us)
Async XLA Ops:
  7.2 321.3 %copy-start = (bf16[1,2048,384]{2,1,0:T(8,128)(2,1)S(1)}, bf16[1,2048,384]{2,1,0:T(8,128)(2,1)}, u32[]{:S(2)}) copy-start(bf16[1,2048,384]{2,1,0:T(8,128)(2,1)} %param.42) | copy-start | bytes 4718596
  9.7 4.7 %copy-start.5 = (bf16[16,2048]{1,0:T(8,128)(2,1)S(1)}, bf16[16,2048]{1,0:T(8,128)(2,1)}, u32[]{:S(2)}) copy-start(bf16[16,2048]{1,0:T(8,128)(2,1)} %param.23) | copy-start | bytes 196612
  9.8 4.8 %copy-start.7 = (s32[16,8]{0,1:T(8,128)S(1)}, s32[16,8]{0,1:T(8,128)}, u32[]{:S(2)}) copy-start(s32[16,8]{0,1:T(8,128)} %param.37) | copy-start | bytes 1540
  11.7 3.1 copy-start.8
  81.2 7.4 %copy-start.2 = (bf16[1,2048,384]{2,1,0:T(8,128)(2,1)S(1)}, bf16[1,2048,384]{2,1,0:T(8,128)(2,1)}, u32[]{:S(2)}) copy-start(bf16[1,2048,384]{2,1,0:T(8,128)(2,1)} %param.31) | copy-start | bytes 4718596
  81.2 33.7 %all-to-all-start.1 = ((bf16[32,8,2,2048]{3,2,0,1:T(2,128)(2,1)}), bf16[32,8,2,2048]{3,2,0,1:T(2,128)(2,1)}, u32[]{:S(2)}, u32[]{:S(2)}) async-start(bf16[32,8,2,2048]{3,2,0,1:T(2,128)(2,1)} %copy.109), calls=%async_computation.1 | async-start | bytes 4194304 | tf_op jit(solution)/shard_map/all_to_all | solution.py:121
  90.7 4.4 %copy-start.12 = (f32[1,16,3]{1,0,2:T(1,128)S(1)}, f32[1,16,3]{1,0,2:T(1,128)}, u32[]{:S(2)}) copy-start(f32[1,16,3]{1,0,2:T(1,128)} %param.32) | copy-start | bytes 580
  90.7 4.4 %copy-start.3 = (bf16[1,2048,384]{2,1,0:T(8,128)(2,1)S(1)}, bf16[1,2048,384]{2,1,0:T(8,128)(2,1)}, u32[]{:S(2)}) copy-start(bf16[1,2048,384]{2,1,0:T(8,128)(2,1)} %param.33) | copy-start | bytes 4718596
  97.2 2.7 copy-start.13
  97.2 2.7 copy-start.14
  97.2 2.9 copy-start.1
  198.7 7.3 %copy-start.9 = (f32[16,8]{0,1:T(8,128)S(1)}, f32[16,8]{0,1:T(8,128)}, u32[]{:S(2)}) copy-start(f32[16,8]{0,1:T(8,128)} %param.38) | copy-start | bytes 1540
  198.7 33.7 %all-to-all-start.3 = ((bf16[32,8,2,2048]{3,2,0,1:T(2,128)(2,1)}), bf16[32,8,2,2048]{3,2,0,1:T(2,128)(2,1)}, u32[]{:S(2)}, u32[]{:S(2)}) async-start(bf16[32,8,2,2048]{3,2,0,1:T(2,128)(2,1)} %copy.113), calls=%async_computation.3 | async-start | bytes 4194304 | tf_op jit(solution)/shard_map/all_to_all | solution.py:133
  206.0 103.2 %all-gather.2.cloned.1.call-start = ((), (), s32[]{:S(2)}) async-start(), calls=%async_computation.6 | async-start | bytes 2162688 | tf_op jit(solution)/shard_map/all_gather | solution.py:147
  236.2 1.2 copy-start.6
  237.3 3.0 copy-start.11
  237.3 3.3 copy-start.10
  237.3 3.3 copy-start.16
  237.4 90.7 %copy-start.4 = (bf16[1,2048,384]{2,1,0:T(8,128)(2,1)S(1)}, bf16[1,2048,384]{2,1,0:T(8,128)(2,1)}, u32[]{:S(2)}) copy-start(bf16[1,2048,384]{2,1,0:T(8,128)(2,1)} %param.41) | copy-start | bytes 4718596
  328.1 7.2 %copy-start.15 = (f32[16,2]{0,1:T(2,128)S(1)}, f32[16,2]{0,1:T(2,128)}, u32[]{:S(2)}) copy-start(f32[16,2]{0,1:T(2,128)} %param.45) | copy-start | bytes 388
  330.9 9.6 %all-to-all-start.5 = ((bf16[8,8,1024]{2,1,0:T(8,128)(2,1)}), bf16[8,8,1024]{2,1,0:T(8,128)(2,1)S(1)}, u32[]{:S(2)}, u32[]{:S(2)}) async-start(bf16[8,8,1024]{2,1,0:T(8,128)(2,1)} %fusion.22), calls=%async_computation.5 | async-start | bytes 262144 | tf_op jit(solution)/shard_map/all_to_all | solution.py:163
Sparse Core Ops, SparseCore 0:
  240.4 68.7 all-gather.1
where the time goes:
time: 349 us; the launch traced here: 348 us
  blocking collectives  130 us (37%)
  waiting for transfers between devices  113 us (32%)
  local copies, waits for them, and re-layouts  44.8 us (13%)
  matrix products  22.4 us (6%)
  starting transfers between devices  19 us (5%)
  between operations  14.3 us (4%)
  other arithmetic  4.66 us (1%)
    all_gather x1, waiting for transfers between devices, local(): gathered = lax.all_gather(thinker_out, 'wide', axis=0, tiled=True)  68.5 us
    all_to_all x1, blocking collectives, local(): lax.all_to_all(doubled, 'wide', split_axis=0, concat_axis=0, tiled=True)  60.3 us
    all_to_all x1, blocking collectives, local(): lax.all_to_all(produced, 'wide', split_axis=0, concat_axis=0, tiled=True)  53.8 us
    all_to_all x1, waiting for transfers between devices, local(): lax.all_to_all(lax.all_to_all(produced, 'wide', split_axis=0, concat_axis...  26.1 us
    all_to_all x1, blocking collectives, local(): lax.all_to_all(talk_outgoing, 'narrow', split_axis=0, concat_axis=0, tile...  15.9 us
    all_to_all x1, waiting for transfers between devices, local(): lax.all_to_all(lax.all_to_all(doubled, 'wide', split_axis=0, concat_axis=...  13 us
    dot_general x2, matrix products, swiglu(): jnp.dot(middle, down_dense, preferred_element_type=jnp.float32)  9.6 us
    unnamed x42, local copies, waits for them, and re-layouts  8.38 us
  transfers between devices with their start and end apart: 4, of which 4 were waited for; matrix products, arithmetic and copies ran while one was open for 4% of the time, Pallas kernels for 0%

commit v1 on v0

--- a/solution.py
+++ b/solution.py
@@ -10,6 +10,9 @@
 TOP = 8
 TTOP = 2
 EPSILON = 1e-06
+see_leaves = lambda x0: jnp.concatenate(
+    lax.all_to_all(jnp.stack([x0] * lax.psum(1, "wide")), "wide", 0, 0), axis=0
+)
 
 
 def dequantize(code_block, scale_block):
@@ -144,7 +147,7 @@
     thinker_out = (residual + routed).astype(jnp.bfloat16)
     own_wide = talker_source // row_count // narrow_count
     own_local = talker_source % row_count
-    gathered = lax.all_gather(thinker_out, "wide", axis=0, tiled=True)
+    gathered = see_leaves(thinker_out)
     talker_in = jnp.take(gathered, own_wide * row_count + own_local, axis=0)
     talker_normed = rms_norm(talker_in, talker_gain)
     talk_capacity = min(row_count, max(2, 2 * row_count * TTOP // narrow_count))

time: 349 us -> 318 us (0.911)
  waiting for transfers between devices: 113 us -> 92.2 us
  between operations: 14.3 us -> 0.9 us
  starting transfers between devices: 19 us -> 24.6 us
  blocking collectives: 130 us -> 126 us
    all_gather x1 -> x0, waiting for transfers between devices: 68.5 us -> none  [local(): gathered = lax.all_gather(thinker_out, 'wide', axis=0, tiled=True)]
    all_to_all x0 -> x1, waiting for transfers between devices: none -> 47.8 us  [lax.all_to_all(jnp.stack([x0] * lax.psum(1, 'wide')), 'wide', 0, 0)]
    all_to_all x0 -> x1, starting transfers between devices: none -> 5.58 us  [lax.all_to_all(jnp.stack([x0] * lax.psum(1, 'wide')), 'wide', 0, 0)]
    all_to_all x1, blocking collectives: 15.9 us -> 11.7 us  [local(): lax.all_to_all(talk_outgoing, 'narrow', split_axis=0, concat_axis=0, tile...]
where the time goes in v1:
time: 318 us; the launch traced here: 317 us
  blocking collectives  126 us (40%)
  waiting for transfers between devices  92.2 us (29%)
  local copies, waits for them, and re-layouts  47.1 us (15%)
  starting transfers between devices  24.6 us (8%)
  matrix products  21.8 us (7%)
  other arithmetic  4.64 us (1%)
    all_to_all x1, blocking collectives, local(): lax.all_to_all(doubled, 'wide', split_axis=0, concat_axis=0, tiled=True)  60.3 us
    all_to_all x1, blocking collectives, local(): lax.all_to_all(produced, 'wide', split_axis=0, concat_axis=0, tiled=True)  53.8 us
    all_to_all x1, waiting for transfers between devices, lax.all_to_all(jnp.stack([x0] * lax.psum(1, 'wide')), 'wide', 0, 0)  47.8 us
    all_to_all x1, waiting for transfers between devices, local(): lax.all_to_all(lax.all_to_all(produced, 'wide', split_axis=0, concat_axis...  26.2 us
    all_to_all x1, waiting for transfers between devices, local(): lax.all_to_all(lax.all_to_all(doubled, 'wide', split_axis=0, concat_axis=...  12.9 us
    all_to_all x1, blocking collectives, local(): lax.all_to_all(talk_outgoing, 'narrow', split_axis=0, concat_axis=0, tile...  11.7 us
    dot_general x2, matrix products, swiglu(): jnp.dot(middle, down_dense, preferred_element_type=jnp.float32)  9.63 us
    unnamed x42, local copies, waits for them, and re-layouts  8.98 us
  transfers between devices with their start and end apart: 4, of which 4 were waited for; matrix products, arithmetic and copies ran while one was open for 4% of the time, Pallas kernels for 0%

profile of v1, /device:TPU:1, one launch (start us, length us, event | category | flops | bytes accessed | tf_op | source)
XLA Modules:
  0.0 317.2 jit_solution(16308003729001815453)
XLA Ops:
  11.2 60.3 %all_to_all.35 = bf16[32,8,2,2048]{3,2,1,0:T(2,128)(2,1)S(1)} all-to-all(bf16[32,8,2,2048]{3,2,1,0:T(2,128)(2,1)S(1)} %bitcast.149), channel_id=1, replica_groups=mesh['wide'=32,'narrow'=8] {'wide'}, dimensions={0} | all-to-all | bytes 4194304 | tf_op jit(solution)/shard_map/all_to_all | solution.py:125
  71.6 3.1 copy.109
  74.6 7.4 %all-to-all-start.1 = ((bf16[32,8,2,2048]{3,2,0,1:T(2,128)(2,1)}), bf16[32,8,2,2048]{3,2,0,1:T(2,128)(2,1)}, u32[]{:S(2)}, u32[]{:S(2)}) async-start(bf16[32,8,2,2048]{3,2,0,1:T(2,128)(2,1)} %copy.109), calls=%async_computation.1 | async-start | bytes 4194304 | tf_op jit(solution)/shard_map/all_to_all | solution.py:124
  84.2 4.3 %copy.130 = f32[48,8,16,128]{3,2,1,0:T(8,128)} copy(f32[48,8,16,128]{3,1,2,0:T(8,128)} %bitcast.147) | data formatting | bytes 6291456
  90.8 2.7 copy.132
  95.4 12.9 %all-to-all-done.1 = bf16[32,8,2,2048]{3,2,0,1:T(2,128)(2,1)} async-done(((bf16[32,8,2,2048]{3,2,0,1:T(2,128)(2,1)}), bf16[32,8,2,2048]{3,2,0,1:T(2,128)(2,1)}, u32[]{:S(2)}, u32[]{:S(2)}) %all-to-all-start.1) | async-done | bytes 2097184 | tf_op jit(solution)/shard_map/all_to_all | solution.py:124
  108.4 5.2 %copy.110 = bf16[32,8,2,2048]{3,2,1,0:T(2,128)(2,1)} copy(bf16[32,8,2,2048]{3,2,0,1:T(2,128)(2,1)} %all-to-all-done.1) | data formatting | bytes 4194304 | tf_op jit(solution)/shard_map/all_to_all | solution.py:124
  113.5 4.1 %reshape.195 = bf16[512,2048]{1,0:T(8,128)(2,1)} reshape(bf16[32,8,2,2048]{3,2,1,0:T(2,128)(2,1)} %copy.110) | data formatting | bytes 4194304 | tf_op jit(solution)/shard_map/reshape | solution.py:134
  117.6 4.2 %fusion.8 = f32[512,384]{1,0:T(8,128)} fusion(bf16[512,2048]{1,0:T(8,128)(2,1)} %reshape.195, bf16[48,8,16,128]{3,2,1,0:T(8,128)(2,1)} %bitcast.153), kind=kOutput, calls=%fused_computation.16 | convolution fusion | flops 805306368 | bytes 4456448 | tf_op jit(solution)/shard_map/dot_general | solution.py:32
  123.8 7.1 %convolution_convert_fusion = bf16[512,2048]{1,0:T(8,128)(2,1)} fusion(f32[48,8,16,128]{3,2,1,0:T(8,128)} %bitcast.151, bf16[1,384,2048]{2,1,0:T(8,128)(2,1)} %param.35, bf16[512,2048]{1,0:T(8,128)(2,1)} %reshape.195, bf16[48,8,16,128]{3,2,1,0:T(8,128)(2,1)S(1)} %bitcast.152, f32[512,384]{1,0:T(8,128)} %fusion.8), kind=kOutput, calls=%fused_computation.5 | convolution fusion | flops 1615200256 | bytes 11272192 | tf_op jit(solution)/shard_map/dot_general | solution.py:35
  131.0 4.4 %reshape.196 = bf16[32,8,2,2048]{3,2,1,0:T(2,128)(2,1)} reshape(bf16[512,2048]{1,0:T(8,128)(2,1)} %convolution_convert_fusion) | data formatting | bytes 4194304 | tf_op jit(solution)/shard_map/reshape | solution.py:135
  135.3 53.8 %all_to_all.36 = bf16[32,8,2,2048]{3,2,1,0:T(2,128)(2,1)S(1)} all-to-all(bf16[32,8,2,2048]{3,2,1,0:T(2,128)(2,1)} %reshape.196), channel_id=1, replica_groups=mesh['wide'=32,'narrow'=8] {'wide'}, dimensions={0} | all-to-all | bytes 4194304 | tf_op jit(solution)/shard_map/all_to_all | solution.py:137
  189.1 3.1 copy.113
  192.2 7.3 %all-to-all-start.3 = ((bf16[32,8,2,2048]{3,2,0,1:T(2,128)(2,1)}), bf16[32,8,2,2048]{3,2,0,1:T(2,128)(2,1)}, u32[]{:S(2)}, u32[]{:S(2)}) async-start(bf16[32,8,2,2048]{3,2,0,1:T(2,128)(2,1)} %copy.113), calls=%async_computation.3 | async-start | bytes 4194304 | tf_op jit(solution)/shard_map/all_to_all | solution.py:136
  199.7 26.2 %all-to-all-done.3 = bf16[32,8,2,2048]{3,2,0,1:T(2,128)(2,1)} async-done(((bf16[32,8,2,2048]{3,2,0,1:T(2,128)(2,1)}), bf16[32,8,2,2048]{3,2,0,1:T(2,128)(2,1)}, u32[]{:S(2)}, u32[]{:S(2)}) %all-to-all-start.3) | async-done | bytes 2097184 | tf_op jit(solution)/shard_map/all_to_all | solution.py:136
  225.9 3.8 %copy.114 = bf16[32,8,2,2048]{3,2,1,0:T(2,128)(2,1)S(1)} copy(bf16[32,8,2,2048]{3,2,0,1:T(2,128)(2,1)} %all-to-all-done.3) | data formatting | bytes 4194304 | tf_op jit(solution)/shard_map/all_to_all | solution.py:136
  230.8 2.2 fusion.2
  235.3 5.6 %all-to-all-start.4 = ((bf16[32,16,2048]{2,1,0:T(8,128)(2,1)}), bf16[32,16,2048]{2,1,0:T(8,128)(2,1)}, u32[]{:S(2)}, u32[]{:S(2)}) async-start(bf16[32,16,2048]{2,1,0:T(8,128)(2,1)} %stack.2), calls=%async_computation.4 | async-start | bytes 4194304 | tf_op jit(solution)/shard_map/all_to_all | solution.py:14
  241.2 47.8 %all-to-all-done.4 = bf16[32,16,2048]{2,1,0:T(8,128)(2,1)} async-done(((bf16[32,16,2048]{2,1,0:T(8,128)(2,1)}), bf16[32,16,2048]{2,1,0:T(8,128)(2,1)}, u32[]{:S(2)}, u32[]{:S(2)}) %all-to-all-start.4) | async-done | bytes 2097184 | tf_op jit(solution)/shard_map/all_to_all | solution.py:14
  289.1 2.5 gather_fusion
  292.1 11.7 %all_to_all.37 = bf16[8,8,2048]{2,1,0:T(8,128)(2,1)S(1)} all-to-all(bf16[8,8,2048]{2,1,0:T(8,128)(2,1)S(1)} %convolution_convert_fusion.2), channel_id=1, replica_groups=mesh['wide'=32,'narrow'=8] {'narrow'}, dimensions={0} | all-to-all | bytes 524288 | tf_op jit(solution)/shard_map/all_to_all | solution.py:161
  304.2 2.5 fusion.22
  306.7 4.3 %all-to-all-start.6 = ((bf16[8,8,1024]{2,1,0:T(8,128)(2,1)}), bf16[8,8,1024]{2,1,0:T(8,128)(2,1)S(1)}, u32[]{:S(2)}, u32[]{:S(2)}) async-start(bf16[8,8,1024]{2,1,0:T(8,128)(2,1)} %fusion.22), calls=%async_computation.6 | async-start | bytes 262144 | tf_op jit(solution)/shard_map/all_to_all | solution.py:166
  311.0 5.3 %all-to-all-done.6 = bf16[8,8,1024]{2,1,0:T(8,128)(2,1)S(1)} async-done(((bf16[8,8,1024]{2,1,0:T(8,128)(2,1)}), bf16[8,8,1024]{2,1,0:T(8,128)(2,1)S(1)}, u32[]{:S(2)}, u32[]{:S(2)}) %all-to-all-start.6) | async-done | bytes 131104 | tf_op jit(solution)/shard_map/all_to_all | solution.py:166
  (84 shorter events, 24.3 us)
Async XLA Ops:
  0.6 303.6 %copy-start = (bf16[1,2048,384]{2,1,0:T(8,128)(2,1)S(1)}, bf16[1,2048,384]{2,1,0:T(8,128)(2,1)}, u32[]{:S(2)}) copy-start(bf16[1,2048,384]{2,1,0:T(8,128)(2,1)} %param.42) | copy-start | bytes 4718596
  3.2 4.7 %copy-start.5 = (bf16[16,2048]{1,0:T(8,128)(2,1)S(1)}, bf16[16,2048]{1,0:T(8,128)(2,1)}, u32[]{:S(2)}) copy-start(bf16[16,2048]{1,0:T(8,128)(2,1)} %param.23) | copy-start | bytes 196612
  3.2 4.8 %copy-start.7 = (s32[16,8]{0,1:T(8,128)S(1)}, s32[16,8]{0,1:T(8,128)}, u32[]{:S(2)}) copy-start(s32[16,8]{0,1:T(8,128)} %param.37) | copy-start | bytes 1540
  5.2 3.1 copy-start.8
  74.6 7.4 %copy-start.2 = (bf16[1,2048,384]{2,1,0:T(8,128)(2,1)S(1)}, bf16[1,2048,384]{2,1,0:T(8,128)(2,1)}, u32[]{:S(2)}) copy-start(bf16[1,2048,384]{2,1,0:T(8,128)(2,1)} %param.31) | copy-start | bytes 4718596
  74.6 33.7 %all-to-all-start.1 = ((bf16[32,8,2,2048]{3,2,0,1:T(2,128)(2,1)}), bf16[32,8,2,2048]{3,2,0,1:T(2,128)(2,1)}, u32[]{:S(2)}, u32[]{:S(2)}) async-start(bf16[32,8,2,2048]{3,2,0,1:T(2,128)(2,1)} %copy.109), calls=%async_computation.1 | async-start | bytes 4194304 | tf_op jit(solution)/shard_map/all_to_all | solution.py:124
  84.2 4.3 %copy-start.12 = (f32[1,16,3]{1,0,2:T(1,128)S(1)}, f32[1,16,3]{1,0,2:T(1,128)}, u32[]{:S(2)}) copy-start(f32[1,16,3]{1,0,2:T(1,128)} %param.32) | copy-start | bytes 580
  84.2 4.3 %copy-start.3 = (bf16[1,2048,384]{2,1,0:T(8,128)(2,1)S(1)}, bf16[1,2048,384]{2,1,0:T(8,128)(2,1)}, u32[]{:S(2)}) copy-start(bf16[1,2048,384]{2,1,0:T(8,128)(2,1)} %param.33) | copy-start | bytes 4718596
  90.8 2.7 copy-start.13
  90.8 2.7 copy-start.14
  90.8 2.9 copy-start.1
  192.2 7.3 %copy-start.9 = (f32[16,8]{0,1:T(8,128)S(1)}, f32[16,8]{0,1:T(8,128)}, u32[]{:S(2)}) copy-start(f32[16,8]{0,1:T(8,128)} %param.38) | copy-start | bytes 1540
  192.2 33.7 %all-to-all-start.3 = ((bf16[32,8,2,2048]{3,2,0,1:T(2,128)(2,1)}), bf16[32,8,2,2048]{3,2,0,1:T(2,128)(2,1)}, u32[]{:S(2)}, u32[]{:S(2)}) async-start(bf16[32,8,2,2048]{3,2,0,1:T(2,128)(2,1)} %copy.113), calls=%async_computation.3 | async-start | bytes 4194304 | tf_op jit(solution)/shard_map/all_to_all | solution.py:136
  233.1 0.6 copy-start.6
  235.3 5.6 %copy-start.11 = (s32[16,2]{0,1:T(2,128)S(1)}, s32[16,2]{0,1:T(2,128)}, u32[]{:S(2)}) copy-start(s32[16,2]{0,1:T(2,128)} %param.44) | copy-start | bytes 388
  235.3 5.9 %copy-start.10 = (bf16[2048]{0:T(1024)(128)(2,1)S(1)}, bf16[2048]{0:T(1024)(128)(2,1)}, u32[]{:S(2)}) copy-start(bf16[2048]{0:T(1024)(128)(2,1)} %param.40) | copy-start | bytes 12292
  235.3 5.9 %copy-start.16 = (s32[16]{0:T(128)S(1)}, s32[16]{0:T(128)}, u32[]{:S(2)}) copy-start(s32[16]{0:T(128)} %param.39) | copy-start | bytes 196
  235.3 68.6 %copy-start.4 = (bf16[1,2048,384]{2,1,0:T(8,128)(2,1)S(1)}, bf16[1,2048,384]{2,1,0:T(8,128)(2,1)}, u32[]{:S(2)}) copy-start(bf16[1,2048,384]{2,1,0:T(8,128)(2,1)} %param.41) | copy-start | bytes 4718596
  235.3 53.8 %all-to-all-start.4 = ((bf16[32,16,2048]{2,1,0:T(8,128)(2,1)}), bf16[32,16,2048]{2,1,0:T(8,128)(2,1)}, u32[]{:S(2)}, u32[]{:S(2)}) async-start(bf16[32,16,2048]{2,1,0:T(8,128)(2,1)} %stack.2), calls=%async_computation.4 | async-start | bytes 4194304 | tf_op jit(solution)/shard_map/all_to_all | solution.py:14
  303.8 7.2 %copy-start.15 = (f32[16,2]{0,1:T(2,128)S(1)}, f32[16,2]{0,1:T(2,128)}, u32[]{:S(2)}) copy-start(f32[16,2]{0,1:T(2,128)} %param.45) | copy-start | bytes 388
  306.7 9.6 %all-to-all-start.6 = ((bf16[8,8,1024]{2,1,0:T(8,128)(2,1)}), bf16[8,8,1024]{2,1,0:T(8,128)(2,1)S(1)}, u32[]{:S(2)}, u32[]{:S(2)}) async-start(bf16[8,8,1024]{2,1,0:T(8,128)(2,1)} %fusion.22), calls=%async_computation.6 | async-start | bytes 262144 | tf_op jit(solution)/shard_map/all_to_all | solution.py:166
